TPU v7x, 32 devices: a whole 2x2x4 slice. The times are simulated.
32 devices in a mesh: peer: 2 (over core), dp: 4 (over y, x), vocab: 4 (over z).
Axes of the slice: x: 2, y: 2, z: 4, core: 2. Of those that a mesh axis runs over, the one named last changes fastest.
Arguments:
- hidden: bfloat16 [2, 2048, 4096], P('peer', 'dp', 'vocab'), may hold values from -400 to 400, as said below
- head_weight: bfloat16 [2, 4096, 32000], P('peer', None, 'vocab'), may hold values from -0.09375 to 0.09375
- targets: int32 [2048], P('dp'), may hold values from 0 to 31999
Outputs:
- hidden_grad: float32 [2, 2048, 4096], P('peer', 'dp', 'vocab')
Inputs may be any that keep to these rules, and one draw needn't show every extreme that they name: `hidden`: finite values.
All inputs are finite; a program needn't handle non-finite values.
Results may differ from a plain program's by a relative error of at most 0.004.
Values may be sent and summed in bfloat16 or wider, within the bound.
A program may use at most 192 MiB of HBM per device.

v0:
```python
import jax
import jax.numpy as jnp
from jax import lax
from jax.sharding import PartitionSpec as P

temper = 2.0
mixing = 0.5
loss_scale = 64.0


def from_partner(x, axis, bit):
    return lax.ppermute(x, axis, [(i, i ^ 1 << bit) for i in range(lax.axis_size(axis))])


def body(hidden, head_weight, targets):
    states = hidden[0]
    weight = head_weight[0]
    local_vocab = weight.shape[1]
    gathered = lax.all_gather(states, "vocab", axis=1, tiled=True)
    logits = jnp.dot(gathered, weight, preferred_element_type=jnp.float32)
    cooled = logits / temper
    local_top = jnp.max(logits, axis=1)
    local_cool = jnp.max(cooled, axis=1)
    top, cool = lax.pmax((local_top, local_cool), "vocab")
    local_total = jnp.sum(jnp.exp(logits - top[:, None]), axis=1)
    local_cool_total = jnp.sum(jnp.exp(cooled - cool[:, None]), axis=1)
    total, cool_total = lax.psum((local_total, local_cool_total), "vocab")
    probs = jnp.exp(logits - top[:, None]) / total[:, None]
    soft = (jnp.exp(cooled - cool[:, None]) / cool_total[:, None]).astype(jnp.bfloat16)
    other_soft = from_partner(soft, "peer", 0)
    column_ids = lax.axis_index("vocab") * local_vocab + jnp.arange(local_vocab, dtype=jnp.int32)
    onehot = (targets[:, None] == column_ids[None, :]).astype(jnp.float32)
    logit_grad = (
        loss_scale
        * (
            probs
            - onehot
            + mixing * temper * (soft.astype(jnp.float32) - other_soft.astype(jnp.float32))
        )
    ).astype(jnp.bfloat16)
    shares = lax.psum_scatter(
        lax.dot_general(
            weight, logit_grad, (((1,), (1,)), ((), ())), preferred_element_type=jnp.float32
        ),
        "vocab",
        scatter_dimension=0,
        tiled=True,
    )
    return shares.T[None]


def solution(mesh):
    return jax.shard_map(
        body,
        mesh=mesh,
        in_specs=(P("peer", "dp", "vocab"), P("peer", None, "vocab"), P("dp")),
        out_specs=P("peer", "dp", "vocab"),
        check_vma=False,
    )
```

profile of v0, /device:TPU:0, one launch (start us, length us, event | category | flops | bytes accessed | tf_op | source)
XLA Modules:
  0.0 387.8 jit_solution(6353445925690982975)
XLA Ops:
  6.5 0.0 all-gather.3.cloned.1.call-start
  6.5 0.7 all-gather.3.cloned.1.call-update
  7.3 0.0 reduce-scatter.2.cloned.1.call-start
  7.3 85.1 %all-gather.3.cloned.1.call-done = bf16[1,512,4096]{2,1,0:T(8,128)(2,1)} async-done(((bf16[1,512,1024]{2,1,0:T(8,128)(2,1)}), bf16[1,512,4096]{2,1,0:T(8,128)(2,1)}) %all-gather.3.cloned.1.call-update) | async-done | bytes 4194320 | tf_op jit(solution)/shard_map/all_gather | solution.py:19
  92.4 42.0 %fusion.16 = (f32[512]{0:T(512)S(1)}, f32[512]{0:T(512)S(1)}, f32[512,8000]{0,1:T(8,128)}) fusion(bf16[1,4096,8000]{1,2,0:T(8,128)(2,1)} %param.4, bf16[1,512,4096]{2,1,0:T(8,128)(2,1)} %all-gather.3.cloned.1.call-done), kind=kOutput, calls=%fused_computation.20 | convolution fusion | flops 33566720000 | bytes 86118400 | tf_op jit(solution)/shard_map/dot_general | solution.py:20
  134.4 8.9 %all-reduce.1 = (f32[512]{0:T(512)S(1)}, f32[512]{0:T(512)S(1)}) all-reduce(f32[512]{0:T(512)S(1)} %get-tuple-element.7, f32[512]{0:T(512)S(1)} %get-tuple-element.8), channel_id=1, replica_groups=mesh['peer'=2,'dp'=4,'vocab'=4] {'vocab'}, use_global_device_ids=true, to_apply=%region_1.0 | all-reduce | flops 1024 | bytes 8192 | tf_op jit(solution)/shard_map/pmax | solution.py:24
  143.4 8.2 %fusion.4 = (f32[512]{0:T(512)S(1)}, f32[512]{0:T(512)S(1)}) fusion(f32[512,8000]{0,1:T(8,128)} %get-tuple-element.13, f32[512]{0:T(512)S(1)} %get-tuple-element.11, f32[512]{0:T(512)S(1)} %get-tuple-element.12), kind=kLoop, calls=%fused_computation.9 | loop fusion | flops 20478976 | bytes 16392192 | tf_op jit(solution)/shard_map/reduce_sum | solution.py:25
  151.6 0.0 copy-start
  151.6 10.0 %all-reduce = (f32[512]{0:T(512)S(1)}, f32[512]{0:T(512)S(1)}) all-reduce(f32[512]{0:T(512)S(1)} %get-tuple-element.6, f32[512]{0:T(512)S(1)} %get-tuple-element.5), channel_id=1, replica_groups=mesh['peer'=2,'dp'=4,'vocab'=4] {'vocab'}, use_global_device_ids=true, to_apply=%region_7.0 | all-reduce | flops 1024 | bytes 8192 | tf_op jit(solution)/shard_map/psum | solution.py:27
  161.6 10.0 %divide_convert_fusion = bf16[512,8000]{0,1:T(8,128)(2,1)} fusion(f32[512,8000]{0,1:T(8,128)} %get-tuple-element.13, f32[512]{0:T(512)S(1)} %get-tuple-element.9, f32[512]{0:T(512)S(1)} %get-tuple-element.12), kind=kLoop, calls=%fused_computation.5 | loop fusion | flops 16384000 | bytes 24580096 | tf_op jit(solution)/shard_map/convert_element_type | solution.py:29
  171.6 0.0 collective-permute-start
  171.6 13.2 %collective-permute-done = bf16[512,8000]{0,1:T(8,128)(2,1)} collective-permute-done((bf16[512,8000]{0,1:T(8,128)(2,1)}, bf16[512,8000]{0,1:T(8,128)(2,1)}, u32[]{:S(2)}, u32[]{:S(2)}) %collective-permute-start) | collective-permute-done | bytes 8192032 | tf_op jit(solution)/shard_map/ppermute | solution.py:12
  184.8 0.0 copy-done
  184.8 53.1 %fusion.11 = f32[4096,512]{0,1:T(8,128)} fusion(bf16[1,4096,8000]{1,2,0:T(8,128)(2,1)} %param.4, bf16[512,8000]{0,1:T(8,128)(2,1)} %collective-permute-done, f32[512,8000]{0,1:T(8,128)} %get-tuple-element.13, s32[512]{0:T(512)S(1)} %copy-done, f32[512]{0:T(512)S(1)} %get-tuple-element.10, f32[512]{0:T(512)S(1)} %get-tuple-element.11, ...), kind=kOutput, calls=%fused_computation.16 | convolution fusion | flops 33615872000 | bytes 98542848 | tf_op jit(solution)/shard_map/dot_general | solution.py:42
  237.9 0.0 reduce-scatter.2.cloned.1.call-update
  238.0 143.0 %reduce-scatter.2.cloned.1.call-done = f32[1024,512]{0,1:T(8,128)} async-done(((f32[4096,512]{0,1:T(8,128)}), f32[1024,512]{0,1:T(8,128)}) %reduce-scatter.2.cloned.1.call-update) | async-done | bytes 2097168 | tf_op jit(solution)/shard_map/reduce_scatter | solution.py:41
  (1 shorter events, 0.0 us)
Async XLA Ops:
  6.5 85.9 %all-gather.3.cloned.1.call-start = ((), (), s32[]{:S(2)}) async-start(), calls=%async_computation.2 | async-start | bytes 5242880 | tf_op jit(solution)/shard_map/all_gather | solution.py:19
  7.3 373.7 %reduce-scatter.2.cloned.1.call-start = ((), (), s32[]{:S(2)}) async-start(), calls=%async_computation.1 | async-start | bytes 10485760 | tf_op jit(solution)/shard_map/reduce_scatter | solution.py:41
  151.6 33.2 %copy-start = (s32[512]{0:T(512)S(1)}, s32[512]{0:T(512)}, u32[]{:S(2)}) copy-start(s32[512]{0:T(512)} %param.5) | copy-start | bytes 6148
  171.6 13.2 %collective-permute-start = (bf16[512,8000]{0,1:T(8,128)(2,1)}, bf16[512,8000]{0,1:T(8,128)(2,1)}, u32[]{:S(2)}, u32[]{:S(2)}) collective-permute-start(bf16[512,8000]{0,1:T(8,128)(2,1)} %divide_convert_fusion), channel_id=1, source_target_pairs={{0,16},{16,0},{1,17},{17,1},{2,18},{18,2},{3,19},{19,3},{4,20},{20... | collective-permute-start | bytes 24576008 | tf_op jit(solution)/shard_map/ppermute | solution.py:12
Sparse Core Ops, SparseCore 0:
  8.9 83.4 all-gather.2
  238.1 142.8 reduce-scatter.1
where the time goes:
time: 388 us
  waiting for transfers between devices  242 us (62%)
  matrix products  95.2 us (25%)
  blocking collectives  18.9 us (5%)
  other arithmetic  18.2 us (5%)
  between operations  13.4 us (3%)
    reduce_scatter x1, waiting for transfers between devices, body(): lax.psum_scatter(lax.dot_general(weight, logit_grad, (((1,), (1,)), ((),...  143 us
    all_gather x1, waiting for transfers between devices, body(): gathered = lax.all_gather(states, 'vocab', axis=1, tiled=True)  85.1 us
    dot_general x1, matrix products, body(): lax.dot_general(weight, logit_grad, (((1,), (1,)), ((), ())), preferred_e...  53.1 us
    dot_general x1, matrix products, body(): logits = jnp.dot(gathered, weight, preferred_element_type=jnp.float32)  42 us
    ppermute x1, waiting for transfers between devices, from_partner(): lax.ppermute(x, axis, [(i, i ^ 1 << bit) for i in range(lax.axis_size(axi...  13.2 us
    convert_element_type x1, other arithmetic, body(): (jnp.exp(cooled - cool[:, None]) / cool_total[:, None]).astype(jnp.bfloat16)  10 us
    psum x1, blocking collectives, body(): total, cool_total = lax.psum((local_total, local_cool_total), 'vocab')  9.97 us
    pmax x1, blocking collectives, body(): top, cool = lax.pmax((local_top, local_cool), 'vocab')  8.93 us
  transfers between devices with their start and end apart: 3, of which 3 were waited for; matrix products, arithmetic and copies ran while one was open for 0% of the time, Pallas kernels for 0%

commit v1 on v0

--- a/solution.py
+++ b/solution.py
@@ -1,18 +1,28 @@
+import functools
+
 import jax
 import jax.numpy as jnp
 from jax import lax
+from jax.experimental import pallas as pl
+from jax.experimental.pallas import tpu as pltpu
 from jax.sharding import PartitionSpec as P
 
 temper = 2.0
 mixing = 0.5
 loss_scale = 64.0
 
+WIRE = jnp.int16
+WIRE_TOP = 32766.0
+PIECES = 2
+LAG = 2
+HALF_LOG2E = 0.7213475204444817
+
 
 def from_partner(x, axis, bit):
     return lax.ppermute(x, axis, [(i, i ^ 1 << bit) for i in range(lax.axis_size(axis))])
 
 
-def body(hidden, head_weight, targets):
+def plain_body(hidden, head_weight, targets):
     states = hidden[0]
     weight = head_weight[0]
     local_vocab = weight.shape[1]
@@ -49,7 +59,377 @@
     return shares.T[None]
 
 
+def kernel(
+    n, hidden_ref, weight_ref, targets_ref, out_ref,
+    held, logits, wbuf, soft, grad, wire, unit, stat, rows_buf,
+    own_sem, wsem, gather_recv, right_sem, left_sem,
+    stat_send, stat_recv, soft_send, soft_recv, wire_send, wire_recv, unit_send, unit_recv, out_sem,
+):
+    z = lax.axis_index("vocab")
+    other = 1 - lax.axis_index("peer")
+    tokens, vocab = logits.shape
+    steps = n * PIECES
+    depth = held.shape[2]
+
+    def remote(src, dst, send, recv, **where):
+        return pltpu.make_async_remote_copy(
+            src_ref=src, dst_ref=dst, send_sem=send, recv_sem=recv,
+            device_id=where, device_id_type=pl.DeviceIdType.MESH,
+        )
+
+    def order(j):
+        both = jnp.minimum(z, n - 1 - z) * PIECES
+        k = j - PIECES
+        paired = k < 2 * both
+        p = jnp.where(paired, lax.div(jnp.maximum(k, 0), 2), k - both)
+        leftward = jnp.where(paired, lax.rem(jnp.maximum(k, 0), 2) == 0, z > n - 1 - z)
+        p = jnp.maximum(p, 0)
+        far = 1 + lax.div(p, PIECES)
+        shard = jnp.where(j < PIECES, z, jnp.where(leftward, z - far, z + far))
+        piece = jnp.where(j < PIECES, j, lax.rem(p, PIECES))
+        return shard, piece, both
+
+    def place(j):
+        shard, piece, _ = order(j)
+        return shard * PIECES + piece
+
+    def load_weight(j, slot):
+        row = pl.multiple_of(place(j) * depth, depth)
+        return pltpu.make_async_copy(
+            weight_ref.at[0, pl.ds(row, depth), :], wbuf.at[slot], wsem.at[slot]
+        )
+
+    def send_right(at):
+        return remote(held.at[at], held.at[at], right_sem.at[at], gather_recv.at[at], vocab=jnp.minimum(z + 1, n - 1))
+
+    def send_left(at):
+        return remote(held.at[at], held.at[at], left_sem.at[at], gather_recv.at[at], vocab=jnp.maximum(z - 1, 0))
+
+    load_weight(0, 0).start()
+    own = [
+        pltpu.make_async_copy(
+            hidden_ref.at[0, :, pl.ds(c * depth, depth)], held.at[z * PIECES + c], own_sem.at[c]
+        )
+        for c in range(PIECES)
+    ]
+    for copy in own:
+        copy.start()
+
+    barrier = pltpu.get_barrier_semaphore()
+    for o in range(1, n):
+        pl.semaphore_signal(
+            barrier, inc=1, device_id={"vocab": lax.rem(z + o, n)}, device_id_type=pl.DeviceIdType.MESH
+        )
+    pl.semaphore_signal(barrier, inc=1, device_id={"peer": other}, device_id_type=pl.DeviceIdType.MESH)
+    pl.semaphore_wait(barrier, n)
+
+    for c in range(PIECES):
+        own[c].wait()
+
+        @pl.when(z < n - 1)
+        def _():
+            send_right(z * PIECES + c).start()
+
+        @pl.when(z > 0)
+        def _():
+            send_left(z * PIECES + c).start()
+
+    block = 32
+
+    @pl.loop(0, tokens // block)
+    def _(r):
+        logits[pl.ds(pl.multiple_of(r * block, block), block), :] = jnp.zeros((block, vocab), jnp.float32)
+
+    def arrive(at, leftward):
+        remote(held.at[at], held.at[at], right_sem.at[at], gather_recv.at[at], peer=other).wait_recv()
+
+        @pl.when(jnp.logical_and(leftward, z < n - 1))
+        def _():
+            send_right(at).start()
+
+        @pl.when(jnp.logical_and(jnp.logical_not(leftward), z > 0))
+        def _():
+            send_left(at).start()
+
+    width = 1024
+    whole = vocab // width
+
+    @pl.loop(0, steps)
+    def _(j):
+        slot = lax.rem(j, 2)
+        shard, piece, both = order(j)
+        at = shard * PIECES + piece
+        k = j - PIECES
+        paired = jnp.logical_and(k >= 0, k < 2 * both)
+        first = jnp.logical_and(paired, lax.rem(jnp.maximum(k, 0), 2) == 0)
+        single = k >= 2 * both
+
+        @pl.when(j + 1 < steps)
+        def _():
+            load_weight(j + 1, 1 - slot).start()
+
+        @pl.when(jnp.logical_and(k >= 0, jnp.logical_or(first, single)))
+        def _():
+            arrive(at, shard < z)
+
+        @pl.when(first)
+        def _():
+            arrive(place(j + 1), jnp.bool_(False))
+
+        load_weight(j, slot).wait()
+        x = held.at[at]
+        w = wbuf.at[slot]
+
+        @pl.loop(0, whole)
+        def _(t):
+            cols = pl.ds(pl.multiple_of(t * width, width), width)
+            logits[:, cols] += jnp.dot(x[...], w[:, cols], preferred_element_type=jnp.float32)
+
+        if whole * width < vocab:
+            cols = pl.ds(whole * width, vocab - whole * width)
+            logits[:, cols] += jnp.dot(x[...], w[:, cols], preferred_element_type=jnp.float32)
+
+    lane = lax.broadcasted_iota(jnp.int32, (block, 128), 1)
+
+    @pl.loop(0, tokens // block)
+    def _(r):
+        rows = pl.ds(pl.multiple_of(r * block, block), block)
+        x = logits[rows, :]
+        top = jnp.max(x, axis=1, keepdims=True)
+        e = jnp.exp2((x - top) * HALF_LOG2E)
+        logits[rows, :] = e
+        cool = jnp.sum(e, axis=1, keepdims=True)
+        total = jnp.sum(e * e, axis=1, keepdims=True)
+        stat[rows, :] = jnp.where(lane == 0, top, jnp.where(lane == 1, total, cool))
+
+    rows_buf[z] = stat[...].T[:8]
+
+    def stat_copy(o):
+        return remote(
+            rows_buf.at[z], rows_buf.at[z], stat_send.at[o], stat_recv.at[z], vocab=lax.rem(z + o, n)
+        )
+
+    for o in range(1, n):
+        stat_copy(o).start()
+    for o in range(1, n):
+        source = lax.rem(z + o, n)
+        remote(rows_buf.at[source], rows_buf.at[source], stat_send.at[o], stat_recv.at[source], peer=other).wait_recv()
+
+    top = rows_buf[0, 0:1, :]
+    for i in range(1, n):
+        top = jnp.maximum(top, rows_buf[i, 0:1, :])
+    total = jnp.zeros_like(top)
+    cool = jnp.zeros_like(top)
+    for i in range(n):
+        shrink = jnp.exp((rows_buf[i, 0:1, :] - top) * 0.5)
+        total += rows_buf[i, 1:2, :] * (shrink * shrink)
+        cool += rows_buf[i, 2:3, :] * shrink
+    shrink = jnp.exp((rows_buf[z, 0:1, :] - top) * 0.5)
+    hard_scale = (shrink * shrink) / total
+    soft_scale = shrink / cool
+    pick = lax.broadcasted_iota(jnp.int32, (128, tokens), 0)
+    stat[...] = jnp.where(pick == 0, hard_scale, soft_scale).T
+
+    group = 64
+    groups = tokens // group
+
+    def soft_copy(r):
+        rows = pl.ds(pl.multiple_of(r * group, group), group)
+        return remote(soft.at[rows, :], grad.at[rows, :], soft_send.at[r], soft_recv.at[r], peer=other)
+
+    @pl.loop(0, groups)
+    def _(r):
+        rows = pl.ds(pl.multiple_of(r * group, group), group)
+        soft[rows, :] = (logits[rows, :] * stat[rows, 1:2]).astype(jnp.bfloat16)
+        soft_copy(r).start()
+
+    sub = 32
+
+    @pl.loop(0, groups)
+    def _(r):
+        soft_copy(r).wait_recv()
+
+        @pl.loop(0, group // sub)
+        def _(q):
+            rows = pl.ds(pl.multiple_of(r * group + q * sub, sub), sub)
+            e = logits[rows, :]
+            ids = lax.broadcasted_iota(jnp.int32, (sub, vocab), 1)
+            onehot = jnp.where(ids == targets_ref[rows, :] - z * vocab, 1.0, 0.0)
+            gap = soft[rows, :].astype(jnp.float32) - grad[rows, :].astype(jnp.float32)
+            full = (e * e) * stat[rows, 0:1] - onehot + (mixing * temper) * gap
+            grad[rows, :] = (loss_scale * full).astype(jnp.bfloat16)
+
+    features = 256
+
+    def columns(at):
+        return pl.ds(pl.multiple_of(at * depth, depth), depth)
+
+    def wire_in(slot):
+        remote(unit.at[slot], unit.at[slot], unit_send.at[0], unit_recv.at[slot], peer=other).wait_recv()
+        remote(wire.at[slot], wire.at[slot], wire_send.at[0], wire_recv.at[slot], peer=other).wait_recv()
+
+    def wire_out(at, dst, target):
+        return (
+            remote(unit.at[at], unit.at[dst], unit_send.at[at], unit_recv.at[dst], vocab=target),
+            remote(wire.at[at], wire.at[dst], wire_send.at[at], wire_recv.at[dst], vocab=target),
+        )
+
+    def wire_start(at, dst, target):
+        for copy in wire_out(at, dst, target):
+            copy.start()
+
+    def out_copy(c):
+        return pltpu.make_async_copy(
+            logits.at[:, columns(z * PIECES + c)], out_ref.at[0, :, pl.ds(c * depth, depth)], out_sem.at[c]
+        )
+
+    def pass_on(i):
+        shard, piece, _ = order(steps - 1 - i)
+        at = shard * PIECES + piece
+        cols = columns(at)
+
+        def add(slot):
+            wire_in(slot)
+            logits[:, cols] += wire[slot].astype(jnp.int32).astype(jnp.float32) * unit[slot, 0:1, :]
+
+        @pl.when(jnp.logical_and(shard <= z, z < n - 1))
+        def _():
+            add(at)
+
+        @pl.when(jnp.logical_and(shard >= z, z > 0))
+        def _():
+            add(jnp.where(shard == z, steps + piece, at))
+
+        @pl.when(shard != z)
+        def _():
+            value = logits[:, cols]
+            peak = jnp.maximum(jnp.max(jnp.abs(value), axis=0, keepdims=True), 1e-30)
+            unit[at] = jnp.broadcast_to(peak * (1.0 / WIRE_TOP), (8, depth))
+            wire[at] = jnp.round(value * (WIRE_TOP / peak)).astype(jnp.int32).astype(WIRE)
+
+        @pl.when(shard < z)
+        def _():
+            wire_start(at, at, jnp.maximum(z - 1, 0))
+
+        @pl.when(shard > z)
+        def _():
+            wire_start(at, jnp.where(shard == z + 1, steps + piece, at), jnp.minimum(z + 1, n - 1))
+
+        @pl.when(shard == z)
+        def _():
+            out_copy(piece).start()
+
+    @pl.loop(0, steps + LAG)
+    def _(i):
+        @pl.when(i < steps)
+        def _():
+            j = steps - 1 - i
+            slot = lax.rem(j, 2)
+            at = place(j)
+
+            @pl.when(i >= 2)
+            def _():
+                load_weight(j, slot).wait()
+
+            @pl.loop(0, depth // features)
+            def _(t):
+                w = wbuf.at[slot, pl.ds(pl.multiple_of(t * features, features), features), :]
+                logits[:, pl.ds(pl.multiple_of(at * depth + t * features, features), features)] = lax.dot_general(
+                    grad[...], w[...], (((1,), (1,)), ((), ())), preferred_element_type=jnp.float32
+                )
+
+            @pl.when(i + 2 < steps)
+            def _():
+                load_weight(j - 2, slot).start()
+
+        @pl.when(i >= LAG)
+        def _():
+            pass_on(i - LAG)
+
+    for at in range(steps):
+        shard = at // PIECES
+
+        @pl.when(jnp.logical_and(shard <= z, z < n - 1))
+        def _():
+            send_right(at).wait_send()
+
+        @pl.when(jnp.logical_and(shard >= z, z > 0))
+        def _():
+            send_left(at).wait_send()
+
+        @pl.when(shard != z)
+        def _():
+            for copy in wire_out(at, at, jnp.where(z > 0, z - 1, 1)):
+                copy.wait_send()
+
+    for o in range(1, n):
+        stat_copy(o).wait_send()
+
+    @pl.loop(0, groups)
+    def _(r):
+        soft_copy(r).wait_send()
+
+    for c in range(PIECES):
+        out_copy(c).wait()
+
+
+def fused_body(n, hidden, head_weight, targets):
+    _, tokens, own = hidden.shape
+    vocab = head_weight.shape[2]
+    depth = own // PIECES
+    steps = n * PIECES
+    dma = pltpu.SemaphoreType.DMA
+    return pl.pallas_call(
+        functools.partial(kernel, n),
+        out_shape=jax.ShapeDtypeStruct((1, tokens, own), jnp.float32),
+        in_specs=[
+            pl.BlockSpec(memory_space=pl.ANY),
+            pl.BlockSpec(memory_space=pl.ANY),
+            pl.BlockSpec(memory_space=pltpu.VMEM),
+        ],
+        out_specs=pl.BlockSpec(memory_space=pl.ANY),
+        scratch_shapes=[
+            pltpu.VMEM((steps, tokens, depth), jnp.bfloat16),
+            pltpu.VMEM((tokens, vocab), jnp.float32),
+            pltpu.VMEM((2, depth, vocab), jnp.bfloat16),
+            pltpu.VMEM((tokens, vocab), jnp.bfloat16),
+            pltpu.VMEM((tokens, vocab), jnp.bfloat16),
+            pltpu.VMEM((steps + PIECES, tokens, depth), WIRE),
+            pltpu.VMEM((steps + PIECES, 8, depth), jnp.float32),
+            pltpu.VMEM((tokens, 128), jnp.float32),
+            pltpu.VMEM((n, 8, tokens), jnp.float32),
+            dma((PIECES,)),
+            dma((2,)),
+            dma((steps,)),
+            dma((steps,)),
+            dma((steps,)),
+            dma((n,)),
+            dma((n,)),
+            dma((tokens // 64,)),
+            dma((tokens // 64,)),
+            dma((steps,)),
+            dma((steps + PIECES,)),
+            dma((steps,)),
+            dma((steps + PIECES,)),
+            dma((PIECES,)),
+        ],
+        compiler_params=pltpu.CompilerParams(
+            collective_id=0, has_side_effects=True, vmem_limit_bytes=63 << 20
+        ),
+    )(hidden, head_weight, targets[:, None])
+
+
 def solution(mesh):
+    n = mesh.shape["vocab"]
+
+    def body(hidden, head_weight, targets):
+        _, tokens, own = hidden.shape
+        vocab = head_weight.shape[2]
+        fits = tokens * vocab * 8 + own * vocab * 2 + tokens * own * n * 4
+        if n > 4 or own % (256 * PIECES) or tokens % 128 or n * own > vocab or fits > 59 << 20:
+            return plain_body(hidden, head_weight, targets)
+        return fused_body(n, hidden, head_weight, targets)
+
     return jax.shard_map(
         body,
         mesh=mesh,

time: 388 us -> 274 us (0.71)
  waiting for transfers between devices: 242 us -> 0 us
  Pallas kernels: 0 us -> 190 us
  matrix products: 95.2 us -> 0 us
  local copies, waits for them, and re-layouts: 0.01 us -> 80.3 us
  blocking collectives: 18.9 us -> 0 us
  other arithmetic: 18.2 us -> 0 us
  between operations: 13.4 us -> 0.01 us
    pallas_call x0 -> x1, Pallas kernels: none -> 190 us  [fused_body(): pl.pallas_call(functools.partial(kernel, n), out_shape=jax.ShapeDtypeStru...]
    reduce_scatter x1 -> x0, waiting for transfers between devices: 143 us -> none  [body(): lax.psum_scatter(lax.dot_general(weight, logit_grad, (((1,), (1,)), ((),...]
    dot_general x2 -> x0, matrix products: 95.2 us -> none  [the longest x1 53.1 us: body(): lax.dot_general(weight, logit_grad, (((1,), (1,)), ((), ())), preferred_e...]
    all_gather x1 -> x0, waiting for transfers between devices: 85.1 us -> none  [body(): gathered = lax.all_gather(states, 'vocab', axis=1, tiled=True)]
    unnamed x2, local copies, waits for them, and re-layouts: 0.01 us -> 78.8 us
    ppermute x1 -> x0, waiting for transfers between devices: 13.2 us -> none  [from_partner(): lax.ppermute(x, axis, [(i, i ^ 1 << bit) for i in range(lax.axis_size(axi...]
    convert_element_type x1 -> x0, other arithmetic: 10 us -> none  [body(): (jnp.exp(cooled - cool[:, None]) / cool_total[:, None]).astype(jnp.bfloat16)]
    psum x1 -> x0, blocking collectives: 9.97 us -> none  [body(): total, cool_total = lax.psum((local_total, local_cool_total), 'vocab')]
  transfers between devices with their start and end apart: 3 -> 0, of which waited for: 3 -> 0; matrix products, arithmetic and copies ran while one was open for 0% -> 0% of each run, Pallas kernels for 0% -> 0%
where the time goes in v1:
time: 274 us; the launch traced here: 271 us
  Pallas kernels  190 us (69%)
  local copies, waits for them, and re-layouts  80.3 us (29%)
    pallas_call x1, Pallas kernels, fused_body(): pl.pallas_call(functools.partial(kernel, n), out_shape=jax.ShapeDtypeStru...  190 us
    unnamed x2, local copies, waits for them, and re-layouts  78.8 us

profile of v1, /device:TPU:0, one launch (start us, length us, event | category | flops | bytes accessed | tf_op | source)
XLA Modules:
  0.0 270.7 jit_solution(6789551699214985224)
XLA Ops:
  0.0 1.5 copy.6.targets_ref
  1.5 75.6 %copy.5.weight_ref = bf16[1,4096,8000]{2,1,0:T(8,128)(2,1)} copy(bf16[1,4096,8000]{1,2,0:T(8,128)(2,1)} %param.4) | data formatting | bytes 131072000 | tf_op args[1]
  77.2 190.4 %shard_map.37 = f32[1,512,1024]{2,1,0:T(8,128)} custom-call(bf16[1,512,1024]{2,1,0:T(8,128)(2,1)} %hidden_ref.1, bf16[1,4096,8000]{2,1,0:T(8,128)(2,1)} %copy.5.weight_ref, s32[512,1]{1,0:T(8,128)} %copy.6.targets_ref), custom_call_target="tpu_custom_call" | custom-call | tf_op jit(solution)/shard_map/pallas_call | solution.py:382
  267.5 3.2 %copy.8 = f32[1,512,1024]{2,1,0:T(8,128)} copy(f32[1,512,1024]{2,1,0:T(8,128)} %shard_map.37) | data formatting | bytes 4194304

commit v2 on v1

--- a/solution.py
+++ b/solution.py
@@ -96,7 +96,7 @@
     def load_weight(j, slot):
         row = pl.multiple_of(place(j) * depth, depth)
         return pltpu.make_async_copy(
-            weight_ref.at[0, pl.ds(row, depth), :], wbuf.at[slot], wsem.at[slot]
+            weight_ref.at[0, :, pl.ds(row, depth)], wbuf.at[slot], wsem.at[slot]
         )
 
     def send_right(at):
@@ -183,11 +183,15 @@
         @pl.loop(0, whole)
         def _(t):
             cols = pl.ds(pl.multiple_of(t * width, width), width)
-            logits[:, cols] += jnp.dot(x[...], w[:, cols], preferred_element_type=jnp.float32)
+            logits[:, cols] += lax.dot_general(
+                x[...], w[cols, :], (((1,), (1,)), ((), ())), preferred_element_type=jnp.float32
+            )
 
         if whole * width < vocab:
             cols = pl.ds(whole * width, vocab - whole * width)
-            logits[:, cols] += jnp.dot(x[...], w[:, cols], preferred_element_type=jnp.float32)
+            logits[:, cols] += lax.dot_general(
+                x[...], w[cols, :], (((1,), (1,)), ((), ())), preferred_element_type=jnp.float32
+            )
 
     lane = lax.broadcasted_iota(jnp.int32, (block, 128), 1)
 
@@ -228,7 +232,8 @@
     hard_scale = (shrink * shrink) / total
     soft_scale = shrink / cool
     pick = lax.broadcasted_iota(jnp.int32, (128, tokens), 0)
-    stat[...] = jnp.where(pick == 0, hard_scale, soft_scale).T
+    local_target = (targets_ref[...] - z * vocab).astype(jnp.float32)
+    stat[...] = jnp.where(pick == 0, hard_scale, jnp.where(pick == 1, soft_scale, local_target)).T
 
     group = 64
     groups = tokens // group
@@ -254,7 +259,7 @@
             rows = pl.ds(pl.multiple_of(r * group + q * sub, sub), sub)
             e = logits[rows, :]
             ids = lax.broadcasted_iota(jnp.int32, (sub, vocab), 1)
-            onehot = jnp.where(ids == targets_ref[rows, :] - z * vocab, 1.0, 0.0)
+            onehot = jnp.where(ids == stat[rows, 2:3].astype(jnp.int32), 1.0, 0.0)
             gap = soft[rows, :].astype(jnp.float32) - grad[rows, :].astype(jnp.float32)
             full = (e * e) * stat[rows, 0:1] - onehot + (mixing * temper) * gap
             grad[rows, :] = (loss_scale * full).astype(jnp.bfloat16)
@@ -333,9 +338,9 @@
 
             @pl.loop(0, depth // features)
             def _(t):
-                w = wbuf.at[slot, pl.ds(pl.multiple_of(t * features, features), features), :]
-                logits[:, pl.ds(pl.multiple_of(at * depth + t * features, features), features)] = lax.dot_general(
-                    grad[...], w[...], (((1,), (1,)), ((), ())), preferred_element_type=jnp.float32
+                w = wbuf[slot, :, pl.ds(pl.multiple_of(t * features, features), features)]
+                logits[:, pl.ds(pl.multiple_of(at * depth + t * features, features), features)] = jnp.dot(
+                    grad[...], w, preferred_element_type=jnp.float32
                 )
 
             @pl.when(i + 2 < steps)
@@ -391,7 +396,7 @@
         scratch_shapes=[
             pltpu.VMEM((steps, tokens, depth), jnp.bfloat16),
             pltpu.VMEM((tokens, vocab), jnp.float32),
-            pltpu.VMEM((2, depth, vocab), jnp.bfloat16),
+            pltpu.VMEM((2, vocab, depth), jnp.bfloat16),
             pltpu.VMEM((tokens, vocab), jnp.bfloat16),
             pltpu.VMEM((tokens, vocab), jnp.bfloat16),
             pltpu.VMEM((steps + PIECES, tokens, depth), WIRE),
@@ -416,7 +421,7 @@
         compiler_params=pltpu.CompilerParams(
             collective_id=0, has_side_effects=True, vmem_limit_bytes=63 << 20
         ),
-    )(hidden, head_weight, targets[:, None])
+    )(hidden, jnp.swapaxes(head_weight, 1, 2), targets[None, :])
 
 
 def solution(mesh):

time: 274 us -> 195 us (0.71)
  local copies, waits for them, and re-layouts: 80.3 us -> 3.16 us
    unnamed x2 -> x1, local copies, waits for them, and re-layouts: 78.8 us -> 3.16 us
where the time goes in v2:
time: 195 us; the launch traced here: 194 us
  Pallas kernels  191 us (98%)
  local copies, waits for them, and re-layouts  3.16 us (2%)
    pallas_call x1, Pallas kernels, fused_body(): pl.pallas_call(functools.partial(kernel, n), out_shape=jax.ShapeDtypeStru...  191 us

profile of v2, /device:TPU:0, one launch (start us, length us, event | category | flops | bytes accessed | tf_op | source)
XLA Modules:
  0.0 193.8 jit_solution(14628769539780983470)
XLA Ops:
  0.0 190.6 %shard_map.37 = f32[1,512,1024]{2,1,0:T(8,128)} custom-call(bf16[1,512,1024]{2,1,0:T(8,128)(2,1)} %hidden_ref.1, bf16[1,8000,4096]{2,1,0:T(8,128)(2,1)} %bitcast.2, s32[1,512]{1,0:T(1,128)} %bitcast.3), custom_call_target="tpu_custom_call" | custom-call | tf_op jit(solution)/shard_map/pallas_call | solution.py:387
  190.6 3.2 %copy.5 = f32[1,512,1024]{2,1,0:T(8,128)} copy(f32[1,512,1024]{2,1,0:T(8,128)} %shard_map.37) | data formatting | bytes 4194304
